TPU v7x, 32 devices: a whole 2x2x4 slice. The times are simulated.
32 devices in a mesh: groups: 2 (over x), bricks: 16 (over z, y, core).
Axes of the slice: x: 2, y: 2, z: 4, core: 2. Of those that a mesh axis runs over, the one named last changes fastest.
Arguments:
- snapshots: bfloat16 [512, 32, 32, 256], P(('groups', 'bricks')), parts along dimension 0, may hold values from -30 to 30
- material: int32 [512, 1024], P(('groups', 'bricks')), parts along dimension 0, may hold values from 0 to 15
- occupancy: int32 [32, 4], P(('groups', 'bricks')), parts along dimension 0, may hold values 0 or 1
- moduli: bfloat16 [16], replicated, may hold values from 0.19921875 to 5
Outputs:
- energy_gram: float32 [512, 256], P(('groups', 'bricks')), parts along dimension 0
There are 2 independent parts, one for each index of `groups`. A program takes and returns all parts, laid end to end along the dimension named above; an argument that names none is the same for every part. Nothing has to cross between parts.
All inputs are finite; a program needn't handle non-finite values. No bound on the sum of `occupancy` on one device may be relied on, other than what follows from the above.
Results may differ from a plain program's by a relative error of at most 0.0003.
Values may be sent and summed in bfloat16 or wider, within the bound.
No kernel may reach another device: no remote copies, remote signals or barrier semaphores. Data moves between devices by JAX's collectives and lax.ppermute only.
A program may use at most 128 MiB of HBM per device.

v0:
```python
import jax
import jax.numpy as jnp
from jax import lax
from jax.sharding import PartitionSpec as P


def with_halo(block, sides, width):
    for axis, dim in sides:
        count = lax.axis_size(axis)
        forward = [(i, i + 1) for i in range(count - 1)]
        backward = [(target, source) for source, target in forward]
        low = lax.ppermute(
            lax.slice_in_dim(block, block.shape[dim] - width, None, axis=dim), axis, forward
        )
        high = lax.ppermute(lax.slice_in_dim(block, 0, width, axis=dim), axis, backward)
        block = jnp.concatenate([low, block, high], axis=dim)
    return block


def stencil(padded_field, padded_modulus):
    depth = padded_field.shape[0] - 2
    rows_y = padded_field.shape[1]
    rows_x = padded_field.shape[2]
    field_full = jnp.pad(padded_field, ((0, 0), (1, 1), (1, 1), (0, 0)))
    modulus_full = jnp.pad(padded_modulus, ((0, 0), (1, 1), (1, 1)))
    center = field_full[1 : 1 + depth, 1 : 1 + rows_y, 1 : 1 + rows_x]
    center_mod = modulus_full[1 : 1 + depth, 1 : 1 + rows_y, 1 : 1 + rows_x]
    mod_sum = jnp.zeros_like(center_mod)
    field_sum = jnp.zeros_like(center)
    product_sum = jnp.zeros_like(center)
    total_weight = 0.0
    for shift_z in (-1, 0, 1):
        for shift_y in (-1, 0, 1):
            for shift_x in (-1, 0, 1):
                nonzero = abs(shift_z) + abs(shift_y) + abs(shift_x)
                if nonzero == 0:
                    continue
                weight = (1.0, 0.5, 0.25)[nonzero - 1]
                total_weight = total_weight + weight
                near = field_full[
                    1 + shift_z : 1 + shift_z + depth,
                    1 + shift_y : 1 + shift_y + rows_y,
                    1 + shift_x : 1 + shift_x + rows_x,
                ]
                near_mod = modulus_full[
                    1 + shift_z : 1 + shift_z + depth,
                    1 + shift_y : 1 + shift_y + rows_y,
                    1 + shift_x : 1 + shift_x + rows_x,
                ]
                mod_sum = mod_sum + weight * near_mod
                field_sum = field_sum + weight * near
                product_sum = product_sum + weight * near_mod[..., None] * near
    diagonal = 0.5 * (total_weight * center_mod + mod_sum)
    return (
        diagonal[..., None] * center - 0.5 * center_mod[..., None] * field_sum - 0.5 * product_sum
    )


def local(snapshots, material, occupancy, moduli):
    depth, rows_y, rows_x, width = snapshots.shape
    owners = lax.axis_size("bricks")
    tiles = occupancy.reshape(rows_y // 16, rows_x // 16)
    occupied = jnp.repeat(jnp.repeat(tiles, 16, 0), 16, 1).astype(jnp.bfloat16)
    classes = jnp.arange(moduli.shape[0], dtype=jnp.int32)
    matches = material[..., None] == classes
    looked = jnp.sum(jnp.where(matches, moduli.astype(jnp.float32), 0.0), axis=-1)
    modulus = looked.astype(jnp.bfloat16).reshape(depth, rows_y, rows_x) * occupied[None]
    field = snapshots * occupied[None, :, :, None]
    padded_field, padded_modulus = (
        with_halo(field, (("bricks", 0),), 1),
        with_halo(modulus, (("bricks", 0),), 1),
    )
    image = stencil(padded_field.astype(jnp.float32), padded_modulus.astype(jnp.float32)).astype(
        jnp.bfloat16
    )
    field_flat = field.reshape(-1, width)
    image_flat = image.reshape(-1, width)
    scale = 1.0 / (depth * rows_y * rows_x * owners)
    own_rows = width // owners
    local_gram = lax.dot_general(
        field_flat, image_flat, (((0,), (0,)), ((), ())), preferred_element_type=jnp.float32
    )
    summed = lax.psum(local_gram, "bricks")
    start = lax.axis_index("bricks") * own_rows
    result = lax.dynamic_slice_in_dim(summed, start, own_rows, 0)
    return result * scale


def solution(mesh):
    in_specs = (
        P(("groups", "bricks"), None, None, None),
        P(("groups", "bricks"), None),
        P(("groups", "bricks"), None),
        P(),
    )
    out_specs = P(("groups", "bricks"), None)
    return jax.shard_map(local, mesh=mesh, in_specs=in_specs, out_specs=out_specs, check_vma=False)
```

profile of v0, /device:TPU:1, one launch (start us, length us, event | category | flops | bytes accessed | tf_op | source)
XLA Modules:
  0.0 343.4 jit_solution(14337007187639578546)
XLA Ops:
  6.5 0.7 convert_reduce_fusion
  7.2 0.1 convert_element_type.46
  7.3 0.1 copy.10
  7.4 0.1 broadcast_in_dim.12
  7.5 0.1 convert_element_type.47
  7.6 0.1 copy.11
  7.7 0.7 convert_element_type.49
  8.3 1.1 select_reduce_fusion
  9.5 0.1 convert_element_type.51
  9.7 4.5 %collective-permute-start = (bf16[1,32,32]{2,1,0:T(8,128)(2,1)S(1)}, bf16[1,32,32]{2,1,0:T(8,128)(2,1)S(1)}, u32[]{:S(2)}, u32[]{:S(2)}) collective-permute-start(bf16[1,32,32]{2,1,0:T(8,128)(2,1)S(1)} %get-tuple-element.35), channel_id=1, source_target_pairs={{0,1},{1,2},{2,3},{3,4},{4,5},{5,6},{6,7},{7,8},{8,9},{9,10},{10,1... | collective-permute-start | bytes 6152 | tf_op jit(solution)/shard_map/ppermute | solution.py:12
  14.2 1.9 collective-permute-start.1
  16.1 8.0 %broadcast_multiply_fusion = bf16[16,32,32,256]{3,2,1,0:T(8,128)(2,1)} fusion(bf16[16,32,32,256]{3,2,1,0:T(8,128)(2,1)} %param.4, bf16[32,32]{1,0:T(8,128)(2,1)S(1)} %copy.11), kind=kLoop, calls=%fused_computation.30 | loop fusion | flops 4194304 | bytes 16779264 | tf_op jit(solution)/shard_map/mul | solution.py:68
  24.2 1.3 fusion.31
  25.4 3.6 %collective-permute-start.2 = (bf16[1,32,32,256]{3,2,1,0:T(8,128)(2,1)S(1)}, bf16[1,32,32,256]{3,2,1,0:T(8,128)(2,1)S(1)}, u32[]{:S(2)}, u32[]{:S(2)}) collective-permute-start(bf16[1,32,32,256]{3,2,1,0:T(8,128)(2,1)S(1)} %get-tuple-element.5), channel_id=1, source_target_pairs={{0,1},{1,2},{2,3},{3,4},{4,5},{5,6},{6,7},{7,8},{8,9},{9,10},{10,1... | collective-permute-start | bytes 1572872 | tf_op jit(solution)/shard_map/ppermute | solution.py:12
  29.1 1.9 collective-permute-start.3
  31.1 2.3 fusion.8
  33.4 3.5 %add_multiply_fusion = (f32[16,32,32]{2,1,0:T(8,128)S(1)}, f32[16,32,32]{2,1,0:T(8,128)S(1)}, f32[16,32,32]{2,1,0:T(8,128)S(1)}, f32[16,32,32]{2,1,0:T(8,128)S(1...) fusion(f32[18,32,32]{2,1,0:T(8,128)S(1)} %maximum_convert_fusion.1), kind=kLoop, calls=%fused_computation.78 | loop fusion | flops 966656 | bytes 2129920 | tf_op jit(solution)/shard_map/mul | solution.py:53
  36.9 2.6 collective-permute-done.3
  39.6 11.4 %maximum_convert_fusion = f32[18,32,32,256]{3,2,1,0:T(8,128)} fusion(bf16[1,32,32,256]{3,2,1,0:T(8,128)(2,1)S(1)} %collective-permute-done.3, bf16[16,32,32,256]{3,2,1,0:T(8,128)(2,1)} %broadcast_multiply_fusion, bf16[1,32,32,256]{3,2,1,0:T(8,128)(2,1)S(1)} %collective-permute-done.2), kind=kLoop, calls=%fused_computation.28 | loop fusion | flops 14155776 | bytes 28311552 | tf_op jit(solution)/shard_map/convert_element_type | solution.py:73
  51.0 184.7 %fusion.37 = bf16[16,32,32,256]{3,2,1,0:T(8,128)(2,1)S(1)} fusion(f32[18,32,32,256]{3,2,1,0:T(8,128)} %maximum_convert_fusion, f32[16,32,32]{2,1,0:T(8,128)} %get-tuple-element.32, f32[16,32,32]{2,1,0:T(8,128)} %get-tuple-element.31, f32[16,32,32]{2,1,0:T(8,128)} %get-tuple-element.30, f32[16,32,32]{2,1,0:T(8,128)} %get-tuple-element.29, ...), kind=kLoop, calls=%fused_computation.27.clone.clone.clone.clone.1 | loop fusion | flops 427819008 | bytes 83951616 | tf_op jit(solution)/shard_map/dot_general | solution.py:80
  235.7 6.5 %fusion.5 = f32[256,256]{1,0:T(8,128)} fusion(bf16[16,32,32,256]{3,2,1,0:T(8,128)(2,1)} %broadcast_multiply_fusion, bf16[16,32,32,256]{3,2,1,0:T(8,128)(2,1)S(1)} %fusion.37), kind=kOutput, calls=%fused_computation.31 | convolution fusion | flops 2147483648 | bytes 17039360 | tf_op jit(solution)/shard_map/dot_general | solution.py:80
  242.1 0.0 all-reduce.4.cloned.1.call-update
  242.2 93.1 %all-reduce.4.cloned.1.call-done = f32[256,256]{1,0:T(8,128)} async-done(((f32[256,256]{1,0:T(8,128)}), f32[256,256]{1,0:T(8,128)}) %all-reduce.4.cloned.1.call-update) | async-done | bytes 262160 | tf_op jit(solution)/shard_map/psum | solution.py:83
  335.2 1.3 dynamic-slice_multiply_fusion
  (8 shorter events, 0.1 us)
Async XLA Ops:
  6.5 328.7 %all-reduce.4.cloned.1.call-start = ((), (), s32[]{:S(2)}) async-start(), calls=%async_computation | async-start | bytes 524288 | tf_op jit(solution)/shard_map/psum | solution.py:83
  9.7 21.4 %collective-permute-start = (bf16[1,32,32]{2,1,0:T(8,128)(2,1)S(1)}, bf16[1,32,32]{2,1,0:T(8,128)(2,1)S(1)}, u32[]{:S(2)}, u32[]{:S(2)}) collective-permute-start(bf16[1,32,32]{2,1,0:T(8,128)(2,1)S(1)} %get-tuple-element.35), channel_id=1, source_target_pairs={{0,1},{1,2},{2,3},{3,4},{4,5},{5,6},{6,7},{7,8},{8,9},{9,10},{10,1... | collective-permute-start | bytes 6152 | tf_op jit(solution)/shard_map/ppermute | solution.py:12
  14.2 16.8 %collective-permute-start.1 = (bf16[1,32,32]{2,1,0:T(8,128)(2,1)S(1)}, bf16[1,32,32]{2,1,0:T(8,128)(2,1)S(1)}, u32[]{:S(2)}, u32[]{:S(2)}) collective-permute-start(bf16[1,32,32]{2,1,0:T(8,128)(2,1)S(1)} %get-tuple-element.36), channel_id=1, source_target_pairs={{1,0},{2,1},{3,2},{4,3},{5,4},{6,5},{7,6},{8,7},{9,8},{10,9},{11,1... | collective-permute-start | bytes 6152 | tf_op jit(solution)/shard_map/ppermute | solution.py:15
  25.4 11.5 %collective-permute-start.2 = (bf16[1,32,32,256]{3,2,1,0:T(8,128)(2,1)S(1)}, bf16[1,32,32,256]{3,2,1,0:T(8,128)(2,1)S(1)}, u32[]{:S(2)}, u32[]{:S(2)}) collective-permute-start(bf16[1,32,32,256]{3,2,1,0:T(8,128)(2,1)S(1)} %get-tuple-element.5), channel_id=1, source_target_pairs={{0,1},{1,2},{2,3},{3,4},{4,5},{5,6},{6,7},{7,8},{8,9},{9,10},{10,1... | collective-permute-start | bytes 1572872 | tf_op jit(solution)/shard_map/ppermute | solution.py:12
  29.1 10.5 %collective-permute-start.3 = (bf16[1,32,32,256]{3,2,1,0:T(8,128)(2,1)S(1)}, bf16[1,32,32,256]{3,2,1,0:T(8,128)(2,1)S(1)}, u32[]{:S(2)}, u32[]{:S(2)}) collective-permute-start(bf16[1,32,32,256]{3,2,1,0:T(8,128)(2,1)S(1)} %get-tuple-element.6), channel_id=1, source_target_pairs={{1,0},{2,1},{3,2},{4,3},{5,4},{6,5},{7,6},{8,7},{9,8},{10,9},{11,1... | collective-permute-start | bytes 1572872 | tf_op jit(solution)/shard_map/ppermute | solution.py:15
Sparse Core Ops, SparseCore 0:
  242.3 92.8 all-reduce.3
where the time goes:
time: 344 us; the launch traced here: 343 us
  other arithmetic  214 us (62%)
  waiting for transfers between devices  95.7 us (28%)
  between operations  13.5 us (4%)
  starting transfers between devices  12 us (3%)
  matrix products  6.48 us (2%)
    dot_general x1, other arithmetic, local(): lax.dot_general(field_flat, image_flat, (((0,), (0,)), ((), ())), preferr...  185 us
    psum x1, waiting for transfers between devices, local(): summed = lax.psum(local_gram, 'bricks')  93.1 us
    convert_element_type x1, other arithmetic, local(): padded_field.astype(jnp.float32)  11.4 us
    ppermute x2, starting transfers between devices, with_halo(): lax.ppermute(lax.slice_in_dim(block, block.shape[dim] - width, None, axis...  8.18 us
    mul x1, other arithmetic, local(): field = snapshots * occupied[None, :, :, None]  8.04 us
  transfers between devices with their start and end apart: 5, of which 2 were waited for; matrix products, arithmetic and copies ran while one was open for 4% of the time, Pallas kernels for 0%

commit v1 on v0

--- a/solution.py
+++ b/solution.py
@@ -80,7 +80,8 @@
     local_gram = lax.dot_general(
         field_flat, image_flat, (((0,), (0,)), ((), ())), preferred_element_type=jnp.float32
     )
-    summed = lax.psum(local_gram, "bricks")
+    parts = lax.all_gather(local_gram, "bricks", axis=0, tiled=False)
+    summed = parts.sum(axis=0)
     start = lax.axis_index("bricks") * own_rows
     result = lax.dynamic_slice_in_dim(summed, start, own_rows, 0)
     return result * scale

time: 344 us -> 307 us (0.89)
  waiting for transfers between devices: 95.7 us -> 57.3 us
    psum x1 -> x0, waiting for transfers between devices: 93.1 us -> none  [local(): summed = lax.psum(local_gram, 'bricks')]
    all_gather x0 -> x1, waiting for transfers between devices: none -> 54.6 us  [local(): parts = lax.all_gather(local_gram, 'bricks', axis=0, tiled=False)]
  transfers between devices with their start and end apart: 5 -> 5, of which waited for: 2 -> 2; matrix products, arithmetic and copies ran while one was open for 4% -> 5% of each run, Pallas kernels for 0% -> 0%
where the time goes in v1:
time: 307 us
  other arithmetic  216 us (70%)
  waiting for transfers between devices  57.3 us (19%)
  between operations  13.5 us (4%)
  starting transfers between devices  12 us (4%)
  matrix products  6.48 us (2%)
    dot_general x1, other arithmetic, local(): lax.dot_general(field_flat, image_flat, (((0,), (0,)), ((), ())), preferr...  185 us
    all_gather x1, waiting for transfers between devices, local(): parts = lax.all_gather(local_gram, 'bricks', axis=0, tiled=False)  54.6 us
    convert_element_type x1, other arithmetic, local(): padded_field.astype(jnp.float32)  11.4 us
    ppermute x2, starting transfers between devices, with_halo(): lax.ppermute(lax.slice_in_dim(block, block.shape[dim] - width, None, axis...  8.18 us
    mul x1, other arithmetic, local(): field = snapshots * occupied[None, :, :, None]  8.04 us
    dot_general x1, matrix products, local(): lax.dot_general(field_flat, image_flat, (((0,), (0,)), ((), ())), preferr...  6.48 us
  transfers between devices with their start and end apart: 5, of which 2 were waited for; matrix products, arithmetic and copies ran while one was open for 5% of the time, Pallas kernels for 0%

profile of v1, /device:TPU:1, one launch (start us, length us, event | category | flops | bytes accessed | tf_op | source)
XLA Modules:
  0.0 306.7 jit_solution(3546975770627629443)
XLA Ops:
  6.5 0.7 convert_reduce_fusion
  7.2 0.1 convert_element_type.46
  7.3 0.1 copy.10
  7.4 0.1 broadcast_in_dim.12
  7.5 0.1 convert_element_type.47
  7.6 0.1 copy.11
  7.7 0.7 convert_element_type.49
  8.3 1.1 select_reduce_fusion
  9.5 0.1 convert_element_type.51
  9.7 4.5 %collective-permute-start = (bf16[1,32,32]{2,1,0:T(8,128)(2,1)S(1)}, bf16[1,32,32]{2,1,0:T(8,128)(2,1)S(1)}, u32[]{:S(2)}, u32[]{:S(2)}) collective-permute-start(bf16[1,32,32]{2,1,0:T(8,128)(2,1)S(1)} %get-tuple-element.35), channel_id=1, source_target_pairs={{0,1},{1,2},{2,3},{3,4},{4,5},{5,6},{6,7},{7,8},{8,9},{9,10},{10,1... | collective-permute-start | bytes 6152 | tf_op jit(solution)/shard_map/ppermute | solution.py:12
  14.2 1.9 collective-permute-start.1
  16.1 8.0 %broadcast_multiply_fusion = bf16[16,32,32,256]{3,2,1,0:T(8,128)(2,1)} fusion(bf16[16,32,32,256]{3,2,1,0:T(8,128)(2,1)} %param.4, bf16[32,32]{1,0:T(8,128)(2,1)S(1)} %copy.11), kind=kLoop, calls=%fused_computation.30 | loop fusion | flops 4194304 | bytes 16779264 | tf_op jit(solution)/shard_map/mul | solution.py:68
  24.2 1.3 fusion.31
  25.4 3.6 %collective-permute-start.2 = (bf16[1,32,32,256]{3,2,1,0:T(8,128)(2,1)S(1)}, bf16[1,32,32,256]{3,2,1,0:T(8,128)(2,1)S(1)}, u32[]{:S(2)}, u32[]{:S(2)}) collective-permute-start(bf16[1,32,32,256]{3,2,1,0:T(8,128)(2,1)S(1)} %get-tuple-element.5), channel_id=1, source_target_pairs={{0,1},{1,2},{2,3},{3,4},{4,5},{5,6},{6,7},{7,8},{8,9},{9,10},{10,1... | collective-permute-start | bytes 1572872 | tf_op jit(solution)/shard_map/ppermute | solution.py:12
  29.1 1.9 collective-permute-start.3
  31.1 2.3 fusion.8
  33.4 3.5 %add_multiply_fusion = (f32[16,32,32]{2,1,0:T(8,128)S(1)}, f32[16,32,32]{2,1,0:T(8,128)S(1)}, f32[16,32,32]{2,1,0:T(8,128)S(1)}, f32[16,32,32]{2,1,0:T(8,128)S(1...) fusion(f32[18,32,32]{2,1,0:T(8,128)S(1)} %maximum_convert_fusion.1), kind=kLoop, calls=%fused_computation.78 | loop fusion | flops 966656 | bytes 2129920 | tf_op jit(solution)/shard_map/mul | solution.py:53
  36.9 2.6 collective-permute-done.3
  39.6 11.4 %maximum_convert_fusion = f32[18,32,32,256]{3,2,1,0:T(8,128)} fusion(bf16[1,32,32,256]{3,2,1,0:T(8,128)(2,1)S(1)} %collective-permute-done.3, bf16[16,32,32,256]{3,2,1,0:T(8,128)(2,1)} %broadcast_multiply_fusion, bf16[1,32,32,256]{3,2,1,0:T(8,128)(2,1)S(1)} %collective-permute-done.2), kind=kLoop, calls=%fused_computation.28 | loop fusion | flops 14155776 | bytes 28311552 | tf_op jit(solution)/shard_map/convert_element_type | solution.py:73
  51.0 184.7 %fusion.37 = bf16[16,32,32,256]{3,2,1,0:T(8,128)(2,1)S(1)} fusion(f32[18,32,32,256]{3,2,1,0:T(8,128)} %maximum_convert_fusion, f32[16,32,32]{2,1,0:T(8,128)} %get-tuple-element.32, f32[16,32,32]{2,1,0:T(8,128)} %get-tuple-element.31, f32[16,32,32]{2,1,0:T(8,128)} %get-tuple-element.30, f32[16,32,32]{2,1,0:T(8,128)} %get-tuple-element.29, ...), kind=kLoop, calls=%fused_computation.27.clone.clone.clone.clone.1 | loop fusion | flops 427819008 | bytes 83951616 | tf_op jit(solution)/shard_map/dot_general | solution.py:80
  235.7 6.5 %fusion.5 = f32[256,256]{1,0:T(8,128)} fusion(bf16[16,32,32,256]{3,2,1,0:T(8,128)(2,1)} %broadcast_multiply_fusion, bf16[16,32,32,256]{3,2,1,0:T(8,128)(2,1)S(1)} %fusion.37), kind=kOutput, calls=%fused_computation.31 | convolution fusion | flops 2147483648 | bytes 17039360 | tf_op jit(solution)/shard_map/dot_general | solution.py:80
  242.2 54.6 %all-gather.3.cloned.1.call-done = f32[4096,256]{1,0:T(8,128)} async-done(((f32[256,256]{1,0:T(8,128)}), f32[4096,256]{1,0:T(8,128)}) %all-gather.3.cloned.1.call-update) | async-done | bytes 4194320 | tf_op jit(solution)/shard_map/all_gather | solution.py:83
  296.8 2.5 reduce_sum.19
  299.2 0.6 dynamic-slice_multiply_fusion
  (9 shorter events, 0.1 us)
Async XLA Ops:
  6.5 290.2 %all-gather.3.cloned.1.call-start = ((), (), s32[]{:S(2)}) async-start(), calls=%async_computation | async-start | bytes 4456448 | tf_op jit(solution)/shard_map/all_gather | solution.py:83
  9.7 21.4 %collective-permute-start = (bf16[1,32,32]{2,1,0:T(8,128)(2,1)S(1)}, bf16[1,32,32]{2,1,0:T(8,128)(2,1)S(1)}, u32[]{:S(2)}, u32[]{:S(2)}) collective-permute-start(bf16[1,32,32]{2,1,0:T(8,128)(2,1)S(1)} %get-tuple-element.35), channel_id=1, source_target_pairs={{0,1},{1,2},{2,3},{3,4},{4,5},{5,6},{6,7},{7,8},{8,9},{9,10},{10,1... | collective-permute-start | bytes 6152 | tf_op jit(solution)/shard_map/ppermute | solution.py:12
  14.2 16.8 %collective-permute-start.1 = (bf16[1,32,32]{2,1,0:T(8,128)(2,1)S(1)}, bf16[1,32,32]{2,1,0:T(8,128)(2,1)S(1)}, u32[]{:S(2)}, u32[]{:S(2)}) collective-permute-start(bf16[1,32,32]{2,1,0:T(8,128)(2,1)S(1)} %get-tuple-element.36), channel_id=1, source_target_pairs={{1,0},{2,1},{3,2},{4,3},{5,4},{6,5},{7,6},{8,7},{9,8},{10,9},{11,1... | collective-permute-start | bytes 6152 | tf_op jit(solution)/shard_map/ppermute | solution.py:15
  25.4 11.5 %collective-permute-start.2 = (bf16[1,32,32,256]{3,2,1,0:T(8,128)(2,1)S(1)}, bf16[1,32,32,256]{3,2,1,0:T(8,128)(2,1)S(1)}, u32[]{:S(2)}, u32[]{:S(2)}) collective-permute-start(bf16[1,32,32,256]{3,2,1,0:T(8,128)(2,1)S(1)} %get-tuple-element.5), channel_id=1, source_target_pairs={{0,1},{1,2},{2,3},{3,4},{4,5},{5,6},{6,7},{7,8},{8,9},{9,10},{10,1... | collective-permute-start | bytes 1572872 | tf_op jit(solution)/shard_map/ppermute | solution.py:12
  29.1 10.5 %collective-permute-start.3 = (bf16[1,32,32,256]{3,2,1,0:T(8,128)(2,1)S(1)}, bf16[1,32,32,256]{3,2,1,0:T(8,128)(2,1)S(1)}, u32[]{:S(2)}, u32[]{:S(2)}) collective-permute-start(bf16[1,32,32,256]{3,2,1,0:T(8,128)(2,1)S(1)} %get-tuple-element.6), channel_id=1, source_target_pairs={{1,0},{2,1},{3,2},{4,3},{5,4},{6,5},{7,6},{8,7},{9,8},{10,9},{11,1... | collective-permute-start | bytes 1572872 | tf_op jit(solution)/shard_map/ppermute | solution.py:15
Sparse Core Ops, SparseCore 0:
  242.3 54.4 all-gather.2
